TPU v7x, 32 devices: a whole 2x2x4 slice. The times are simulated.
32 devices in a mesh: ctx: 8 (over y, x, core), head: 4 (over z).
Axes of the slice: x: 2, y: 2, z: 4, core: 2. Of those that a mesh axis runs over, the one named last changes fastest.
Arguments:
- q_nope: bfloat16 [512, 8192], P('ctx', 'head'), may hold values from -0.59765625 to 0.59765625
- q_rope: bfloat16 [512, 4096], P('ctx', 'head'), may hold values from -6 to 6
- w_uk: bfloat16 [64, 128, 512], P('head'), may hold values from -0.5 to 0.5
- w_uv: bfloat16 [64, 512, 128], P('head'), may hold values from -0.25 to 0.25
- w_o: bfloat16 [8192, 7168], P('head'), may hold values from -0.0625 to 0.0625
- latent_cache: bfloat16 [576, 8192], P(None, 'ctx'), may hold values from -36 to 36
- group_start: int32 [1], replicated, may hold values from 2048 to 7680
Outputs:
- attention_out: bfloat16 [512, 7168], P('ctx', 'head')
All inputs are finite; a program needn't handle non-finite values.
Results may differ from a plain program's by a relative error of at most 0.02.
Values may be sent and summed in bfloat16 or wider, within the bound.
A program may use at most 128 MiB of HBM per device.

v0:
```python
import math
import jax
import jax.numpy as jnp
from jax import lax
from jax.sharding import PartitionSpec as P

LATENT = 512
ROPE = 64
NOPE = 128
VDIM = 128
masked_score = -1e30


def score_scale():
    return (NOPE + ROPE) ** (-0.5) * (0.1 * math.log(32.0) + 1.0) ** 2


def absorb_queries(q_nope, q_rope, w_uk):
    local_heads = w_uk.shape[0]
    tokens_here = q_nope.shape[0]
    nope_part = q_nope.reshape(tokens_here, local_heads, NOPE)
    latent_query = jnp.einsum(
        "thn,hnl->thl", nope_part, w_uk, preferred_element_type=jnp.float32
    ).astype(jnp.bfloat16)
    rope_part = q_rope.reshape(tokens_here, local_heads, ROPE)
    return jnp.concatenate([latent_query, rope_part], axis=2)


def block_scores_of(query_rows, row_position, key_block, key_start):
    scores = jnp.dot(query_rows, key_block, preferred_element_type=jnp.float32) * score_scale()
    key_position = key_start + jnp.arange(key_block.shape[1], dtype=jnp.int32)
    visible = key_position[None, :] <= row_position[:, None]
    return (jnp.where(visible, scores, masked_score), visible)


def latent_product(weights, key_block):
    return lax.dot_general(
        weights.astype(jnp.bfloat16),
        key_block[:LATENT],
        (((1,), (1,)), ((), ())),
        preferred_element_type=jnp.float32,
    )


def online_update(running, query_rows, row_position, key_block, key_start):
    best_sofar, denominator, numerator = running
    scores, visible = block_scores_of(query_rows, row_position, key_block, key_start)
    new_best = jnp.maximum(best_sofar, jnp.max(scores, axis=1))
    decay_factor = jnp.exp(best_sofar - new_best)
    weights = jnp.where(visible, jnp.exp(scores - new_best[:, None]), 0.0)
    denominator = denominator * decay_factor + jnp.sum(weights, axis=1)
    numerator = numerator * decay_factor[:, None] + latent_product(weights, key_block)
    return (new_best, denominator, numerator)


def value_heads(latent_out, w_uv):
    leading = latent_out.astype(jnp.bfloat16)
    remainder = (latent_out - leading.astype(jnp.float32)).astype(jnp.bfloat16)
    first_term = jnp.einsum("thl,hlv->thv", leading, w_uv, preferred_element_type=jnp.float32)
    second_term = jnp.einsum("thl,hlv->thv", remainder, w_uv, preferred_element_type=jnp.float32)
    return first_term + second_term


def on_device(q_nope, q_rope, w_uk, w_uv, w_o, latent_cache, group_start):
    local_heads = w_uk.shape[0]
    tokens_here = q_nope.shape[0]
    queries = absorb_queries(q_nope, q_rope, w_uk)
    query_width = queries.shape[2]
    query_rows = queries.reshape(tokens_here * local_heads, query_width)
    first_token = group_start[0] + lax.axis_index("ctx") * tokens_here
    token_position = first_token + jnp.arange(tokens_here, dtype=jnp.int32)
    row_position = jnp.repeat(token_position, local_heads)
    last_position = first_token + tokens_here - 1
    row_total = query_rows.shape[0]
    initial = (
        jnp.full((row_total,), masked_score, jnp.float32),
        jnp.zeros((row_total,), jnp.float32),
        jnp.zeros((row_total, LATENT), jnp.float32),
    )
    cache_piece = lax.all_gather(latent_cache, "ctx", axis=1, tiled=True)
    span_keys = cache_piece.shape[1]
    step_keys = math.gcd(span_keys, 1024)

    def advance(position, current):
        key_block = lax.dynamic_slice_in_dim(cache_piece, position * step_keys, step_keys, 1)
        key_start = position * step_keys
        return lax.cond(
            key_start <= last_position,
            lambda held_state: online_update(
                held_state, query_rows, row_position, key_block, key_start
            ),
            lambda held_state: held_state,
            current,
        )

    best_all, denominator, numerator = lax.fori_loop(0, span_keys // step_keys, advance, initial)
    latent_out = (numerator / denominator[:, None]).reshape(tokens_here, local_heads, LATENT)
    head_values = value_heads(latent_out, w_uv)
    head_out = head_values.reshape(tokens_here, local_heads * VDIM).astype(jnp.bfloat16)
    mixed_columns = lax.psum_scatter(
        lax.dot_general(
            w_o, head_out, (((0,), (1,)), ((), ())), preferred_element_type=jnp.float32
        ).astype(jnp.bfloat16),
        "head",
        scatter_dimension=0,
        tiled=True,
    ).astype(jnp.float32)
    return mixed_columns.T.astype(jnp.bfloat16)


def solution(mesh):
    placed = (
        P("ctx", "head"),
        P("ctx", "head"),
        P("head", None, None),
        P("head", None, None),
        P("head", None),
        P(None, "ctx"),
        P(),
    )
    return jax.shard_map(
        on_device, mesh=mesh, in_specs=placed, out_specs=P("ctx", "head"), check_vma=False
    )
```

profile of v0, /device:TPU:0, one launch (start us, length us, event | category | flops | bytes accessed | tf_op | source)
XLA Modules:
  0.0 189.2 jit_solution(10341991162294786922)
XLA Ops:
  6.5 0.7 all-gather.2.cloned.1.call-update
  7.3 0.0 reduce-scatter.2.cloned.1.call-start
  8.0 1.1 concatenate.9
  9.1 1.4 fusion.20
  10.5 0.6 copy.12
  11.1 1.2 pad_maximum_fusion
  12.3 58.4 %all-gather.2.cloned.1.call-done = bf16[576,8192]{1,0:T(8,128)(2,1)} async-done(((bf16[576,1024]{1,0:T(8,128)(2,1)}), bf16[576,8192]{1,0:T(8,128)(2,1)}) %all-gather.2.cloned.1.call-update) | async-done | bytes 9437200 | tf_op jit(solution)/shard_map/all_gather | solution.py:80
  70.7 1.6 broadcast_in_dim.29
  72.3 57.2 %while.18 = (s32[]{:T(128)}, f32[1024]{0:T(1024)S(1)}, f32[1024]{0:T(1024)S(1)}, f32[1024,512]{1,0:T(8,128)}, s32[]{:T(128)}, /*index=5*/bf16[576,8192]{1,0:T(8,...) while((s32[]{:T(128)}, f32[1024]{0:T(1024)S(1)}, ...), condition=%wide.region_5.6_spmd.clone, body=%wide.region_0.5_spmd.clone.sunk | while | flops 2299530240 | bytes 37069400 | solution.py:96
  72.3 9.5 %conditional.3 = ((f32[1024]{0:T(1024)S(1)}, f32[1024]{0:T(1024)S(1)}, f32[1024,512]{1,0:T(8,128)})) conditional(s32[]{:T(128)} %convert_element_type.82, (f32[1024]{0:T(1024)S(1)}, f32[1024]{0:T(1024)S(1)}, f32[1024,512]{1,0:T(8,128)}) %tuple.50, (s32[]{:T(128)}, s32[64]{0:T(128)S(1)}, bf16[576,8192]{1,0:T(8,128)(2,1)}, ...), branch_computations={%region_1.0_spmd, %region_2.4_spmd} | conditional | flops 2299530240 | bytes 37069192 | solution.py:87
  72.3 0.1 broadcast_in_dim.35
  72.3 0.1 le.27
  72.4 3.4 %fusion.2 = (f32[1024]{0:T(1024)S(1)}, f32[1024,1024]{1,0:T(8,128)S(1)}) fusion(s32[1024]{0:T(1024)S(1)} %le.27, s32[1024]{0:T(1024)S(1)} %iota_add_fusion, bf16[1024,576]{1,0:T(8,128)(2,1)S(1)} %get-tuple-element.214, bf16[576,8192]{1,0:T(8,128)(2,1)} %get-tuple-element.213, s32[]{:T(128)S(6)} %select_n.18), kind=kOutput, calls=%fused_computation.3 | convolution fusion | flops 1212152832 | bytes 6565892 | tf_op jit(solution)/shard_map/while/body/eval_jaxpr/cond/branch_1_fun/dot_general | solution.py:30
  75.9 1.5 fusion.4
  77.5 0.0 copy-done.1
  77.5 3.0 %multiply_add_fusion = f32[1024,512]{1,0:T(8,128)S(1)} fusion(f32[1024,512]{1,0:T(8,128)S(1)} %copy-done.1, f32[1024,1024]{1,0:T(8,128)S(1)} %get-tuple-element.275, f32[1024]{0:T(1024)S(1)} %max.4, s32[1024]{0:T(1024)S(1)} %le.27, s32[1024]{0:T(1024)S(1)} %iota_add_fusion, bf16[576,8192]{1,0:T(8,128)(2,1)} %get-tuple-element.213, s32[]{:T(128)S(6)} %select_n.18, ...), kind=kOutput, calls=%fused_computation.6 | convolution fusion | flops 1081081856 | bytes 9453572 | tf_op jit(solution)/shard_map/while/body/eval_jaxpr/cond/branch_1_fun/dot_general | solution.py:37
  80.5 1.3 copy-done.2
  81.8 9.5 %conditional.3 = ((f32[1024]{0:T(1024)S(1)}, f32[1024]{0:T(1024)S(1)}, f32[1024,512]{1,0:T(8,128)})) conditional(s32[]{:T(128)} %convert_element_type.82, (f32[1024]{0:T(1024)S(1)}, f32[1024]{0:T(1024)S(1)}, f32[1024,512]{1,0:T(8,128)}) %tuple.50, (s32[]{:T(128)}, s32[64]{0:T(128)S(1)}, bf16[576,8192]{1,0:T(8,128)(2,1)}, ...), branch_computations={%region_1.0_spmd, %region_2.4_spmd} | conditional | flops 2299530240 | bytes 37069192 | solution.py:87
  81.8 0.1 broadcast_in_dim.35
  81.9 0.1 le.27
  82.0 3.4 %fusion.2 = (f32[1024]{0:T(1024)S(1)}, f32[1024,1024]{1,0:T(8,128)S(1)}) fusion(s32[1024]{0:T(1024)S(1)} %le.27, s32[1024]{0:T(1024)S(1)} %iota_add_fusion, bf16[1024,576]{1,0:T(8,128)(2,1)S(1)} %get-tuple-element.214, bf16[576,8192]{1,0:T(8,128)(2,1)} %get-tuple-element.213, s32[]{:T(128)S(6)} %select_n.18), kind=kOutput, calls=%fused_computation.3 | convolution fusion | flops 1212152832 | bytes 6565892 | tf_op jit(solution)/shard_map/while/body/eval_jaxpr/cond/branch_1_fun/dot_general | solution.py:30
  85.4 1.5 fusion.4
  87.0 0.0 copy-done.1
  87.0 3.0 %multiply_add_fusion = f32[1024,512]{1,0:T(8,128)S(1)} fusion(f32[1024,512]{1,0:T(8,128)S(1)} %copy-done.1, f32[1024,1024]{1,0:T(8,128)S(1)} %get-tuple-element.275, f32[1024]{0:T(1024)S(1)} %max.4, s32[1024]{0:T(1024)S(1)} %le.27, s32[1024]{0:T(1024)S(1)} %iota_add_fusion, bf16[576,8192]{1,0:T(8,128)(2,1)} %get-tuple-element.213, s32[]{:T(128)S(6)} %select_n.18, ...), kind=kOutput, calls=%fused_computation.6 | convolution fusion | flops 1081081856 | bytes 9453572 | tf_op jit(solution)/shard_map/while/body/eval_jaxpr/cond/branch_1_fun/dot_general | solution.py:37
  90.0 1.3 copy-done.2
  91.3 9.5 %conditional.3 = ((f32[1024]{0:T(1024)S(1)}, f32[1024]{0:T(1024)S(1)}, f32[1024,512]{1,0:T(8,128)})) conditional(s32[]{:T(128)} %convert_element_type.82, (f32[1024]{0:T(1024)S(1)}, f32[1024]{0:T(1024)S(1)}, f32[1024,512]{1,0:T(8,128)}) %tuple.50, (s32[]{:T(128)}, s32[64]{0:T(128)S(1)}, bf16[576,8192]{1,0:T(8,128)(2,1)}, ...), branch_computations={%region_1.0_spmd, %region_2.4_spmd} | conditional | flops 2299530240 | bytes 37069192 | solution.py:87
  91.4 0.1 broadcast_in_dim.35
  91.4 0.1 le.27
  91.5 3.4 %fusion.2 = (f32[1024]{0:T(1024)S(1)}, f32[1024,1024]{1,0:T(8,128)S(1)}) fusion(s32[1024]{0:T(1024)S(1)} %le.27, s32[1024]{0:T(1024)S(1)} %iota_add_fusion, bf16[1024,576]{1,0:T(8,128)(2,1)S(1)} %get-tuple-element.214, bf16[576,8192]{1,0:T(8,128)(2,1)} %get-tuple-element.213, s32[]{:T(128)S(6)} %select_n.18), kind=kOutput, calls=%fused_computation.3 | convolution fusion | flops 1212152832 | bytes 6565892 | tf_op jit(solution)/shard_map/while/body/eval_jaxpr/cond/branch_1_fun/dot_general | solution.py:30
  95.0 1.5 fusion.4
  96.5 0.0 copy-done.1
  96.6 3.0 %multiply_add_fusion = f32[1024,512]{1,0:T(8,128)S(1)} fusion(f32[1024,512]{1,0:T(8,128)S(1)} %copy-done.1, f32[1024,1024]{1,0:T(8,128)S(1)} %get-tuple-element.275, f32[1024]{0:T(1024)S(1)} %max.4, s32[1024]{0:T(1024)S(1)} %le.27, s32[1024]{0:T(1024)S(1)} %iota_add_fusion, bf16[576,8192]{1,0:T(8,128)(2,1)} %get-tuple-element.213, s32[]{:T(128)S(6)} %select_n.18, ...), kind=kOutput, calls=%fused_computation.6 | convolution fusion | flops 1081081856 | bytes 9453572 | tf_op jit(solution)/shard_map/while/body/eval_jaxpr/cond/branch_1_fun/dot_general | solution.py:37
  99.6 1.3 copy-done.2
  100.9 9.5 %conditional.3 = ((f32[1024]{0:T(1024)S(1)}, f32[1024]{0:T(1024)S(1)}, f32[1024,512]{1,0:T(8,128)})) conditional(s32[]{:T(128)} %convert_element_type.82, (f32[1024]{0:T(1024)S(1)}, f32[1024]{0:T(1024)S(1)}, f32[1024,512]{1,0:T(8,128)}) %tuple.50, (s32[]{:T(128)}, s32[64]{0:T(128)S(1)}, bf16[576,8192]{1,0:T(8,128)(2,1)}, ...), branch_computations={%region_1.0_spmd, %region_2.4_spmd} | conditional | flops 2299530240 | bytes 37069192 | solution.py:87
  100.9 0.1 broadcast_in_dim.35
  101.0 0.1 le.27
  101.0 3.4 %fusion.2 = (f32[1024]{0:T(1024)S(1)}, f32[1024,1024]{1,0:T(8,128)S(1)}) fusion(s32[1024]{0:T(1024)S(1)} %le.27, s32[1024]{0:T(1024)S(1)} %iota_add_fusion, bf16[1024,576]{1,0:T(8,128)(2,1)S(1)} %get-tuple-element.214, bf16[576,8192]{1,0:T(8,128)(2,1)} %get-tuple-element.213, s32[]{:T(128)S(6)} %select_n.18), kind=kOutput, calls=%fused_computation.3 | convolution fusion | flops 1212152832 | bytes 6565892 | tf_op jit(solution)/shard_map/while/body/eval_jaxpr/cond/branch_1_fun/dot_general | solution.py:30
  104.5 1.5 fusion.4
  106.1 0.0 copy-done.1
  106.1 3.0 %multiply_add_fusion = f32[1024,512]{1,0:T(8,128)S(1)} fusion(f32[1024,512]{1,0:T(8,128)S(1)} %copy-done.1, f32[1024,1024]{1,0:T(8,128)S(1)} %get-tuple-element.275, f32[1024]{0:T(1024)S(1)} %max.4, s32[1024]{0:T(1024)S(1)} %le.27, s32[1024]{0:T(1024)S(1)} %iota_add_fusion, bf16[576,8192]{1,0:T(8,128)(2,1)} %get-tuple-element.213, s32[]{:T(128)S(6)} %select_n.18, ...), kind=kOutput, calls=%fused_computation.6 | convolution fusion | flops 1081081856 | bytes 9453572 | tf_op jit(solution)/shard_map/while/body/eval_jaxpr/cond/branch_1_fun/dot_general | solution.py:37
  109.1 1.3 copy-done.2
  110.4 9.5 %conditional.3 = ((f32[1024]{0:T(1024)S(1)}, f32[1024]{0:T(1024)S(1)}, f32[1024,512]{1,0:T(8,128)})) conditional(s32[]{:T(128)} %convert_element_type.82, (f32[1024]{0:T(1024)S(1)}, f32[1024]{0:T(1024)S(1)}, f32[1024,512]{1,0:T(8,128)}) %tuple.50, (s32[]{:T(128)}, s32[64]{0:T(128)S(1)}, bf16[576,8192]{1,0:T(8,128)(2,1)}, ...), branch_computations={%region_1.0_spmd, %region_2.4_spmd} | conditional | flops 2299530240 | bytes 37069192 | solution.py:87
  110.4 0.1 broadcast_in_dim.35
  110.5 0.1 le.27
  110.6 3.4 %fusion.2 = (f32[1024]{0:T(1024)S(1)}, f32[1024,1024]{1,0:T(8,128)S(1)}) fusion(s32[1024]{0:T(1024)S(1)} %le.27, s32[1024]{0:T(1024)S(1)} %iota_add_fusion, bf16[1024,576]{1,0:T(8,128)(2,1)S(1)} %get-tuple-element.214, bf16[576,8192]{1,0:T(8,128)(2,1)} %get-tuple-element.213, s32[]{:T(128)S(6)} %select_n.18), kind=kOutput, calls=%fused_computation.3 | convolution fusion | flops 1212152832 | bytes 6565892 | tf_op jit(solution)/shard_map/while/body/eval_jaxpr/cond/branch_1_fun/dot_general | solution.py:30
  114.0 1.5 fusion.4
  115.6 0.0 copy-done.1
  115.6 3.0 %multiply_add_fusion = f32[1024,512]{1,0:T(8,128)S(1)} fusion(f32[1024,512]{1,0:T(8,128)S(1)} %copy-done.1, f32[1024,1024]{1,0:T(8,128)S(1)} %get-tuple-element.275, f32[1024]{0:T(1024)S(1)} %max.4, s32[1024]{0:T(1024)S(1)} %le.27, s32[1024]{0:T(1024)S(1)} %iota_add_fusion, bf16[576,8192]{1,0:T(8,128)(2,1)} %get-tuple-element.213, s32[]{:T(128)S(6)} %select_n.18, ...), kind=kOutput, calls=%fused_computation.6 | convolution fusion | flops 1081081856 | bytes 9453572 | tf_op jit(solution)/shard_map/while/body/eval_jaxpr/cond/branch_1_fun/dot_general | solution.py:37
  118.7 1.3 copy-done.2
  120.0 9.5 %conditional.3 = ((f32[1024]{0:T(1024)S(1)}, f32[1024]{0:T(1024)S(1)}, f32[1024,512]{1,0:T(8,128)})) conditional(s32[]{:T(128)} %convert_element_type.82, (f32[1024]{0:T(1024)S(1)}, f32[1024]{0:T(1024)S(1)}, f32[1024,512]{1,0:T(8,128)}) %tuple.50, (s32[]{:T(128)}, s32[64]{0:T(128)S(1)}, bf16[576,8192]{1,0:T(8,128)(2,1)}, ...), branch_computations={%region_1.0_spmd, %region_2.4_spmd} | conditional | flops 2299530240 | bytes 37069192 | solution.py:87
  120.0 0.1 broadcast_in_dim.35
  120.0 0.1 le.27
  120.1 3.4 %fusion.2 = (f32[1024]{0:T(1024)S(1)}, f32[1024,1024]{1,0:T(8,128)S(1)}) fusion(s32[1024]{0:T(1024)S(1)} %le.27, s32[1024]{0:T(1024)S(1)} %iota_add_fusion, bf16[1024,576]{1,0:T(8,128)(2,1)S(1)} %get-tuple-element.214, bf16[576,8192]{1,0:T(8,128)(2,1)} %get-tuple-element.213, s32[]{:T(128)S(6)} %select_n.18), kind=kOutput, calls=%fused_computation.3 | convolution fusion | flops 1212152832 | bytes 6565892 | tf_op jit(solution)/shard_map/while/body/eval_jaxpr/cond/branch_1_fun/dot_general | solution.py:30
  123.6 1.5 fusion.4
  125.2 0.0 copy-done.1
  125.2 3.0 %multiply_add_fusion = f32[1024,512]{1,0:T(8,128)S(1)} fusion(f32[1024,512]{1,0:T(8,128)S(1)} %copy-done.1, f32[1024,1024]{1,0:T(8,128)S(1)} %get-tuple-element.275, f32[1024]{0:T(1024)S(1)} %max.4, s32[1024]{0:T(1024)S(1)} %le.27, s32[1024]{0:T(1024)S(1)} %iota_add_fusion, bf16[576,8192]{1,0:T(8,128)(2,1)} %get-tuple-element.213, s32[]{:T(128)S(6)} %select_n.18, ...), kind=kOutput, calls=%fused_computation.6 | convolution fusion | flops 1081081856 | bytes 9453572 | tf_op jit(solution)/shard_map/while/body/eval_jaxpr/cond/branch_1_fun/dot_general | solution.py:37
  128.2 1.3 copy-done.2
  129.5 1.9 %broadcast_divide_fusion = f32[1024,512]{1,0:T(8,128)S(1)} fusion(f32[1024,512]{1,0:T(8,128)} %get-tuple-element.231, f32[1024]{0:T(1024)S(1)} %get-tuple-element.232), kind=kLoop, calls=%fused_computation.31 | loop fusion | flops 524288 | bytes 4198400 | tf_op jit(solution)/shard_map/div | solution.py:97
  131.5 0.3 copy-done.3
  131.7 1.3 fusion.19
  133.0 1.3 fusion.22
  134.4 13.1 %fusion.18 = bf16[7168,64]{0,1:T(8,128)(2,1)} fusion(bf16[2048,7168]{1,0:T(8,128)(2,1)} %param.15, bf16[16,8,8,128]{3,2,1,0:T(8,128)(2,1)S(1)} %fusion.22), kind=kOutput, calls=%fused_computation.21 | convolution fusion | flops 1879506944 | bytes 30539776 | tf_op jit(solution)/shard_map/dot_general | solution.py:101
  147.4 0.0 reduce-scatter.2.cloned.1.call-update
  147.5 34.9 %reduce-scatter.2.cloned.1.call-done = bf16[1792,64]{0,1:T(8,128)(2,1)} async-done(((bf16[7168,64]{0,1:T(8,128)(2,1)}), bf16[1792,64]{0,1:T(8,128)(2,1)}) %reduce-scatter.2.cloned.1.call-update) | async-done | bytes 229392 | tf_op jit(solution)/shard_map/reduce_scatter | solution.py:100
  (47 shorter events, 0.2 us)
Async XLA Ops:
  6.5 2.5 %copy-start = (bf16[16,128,512]{2,1,0:T(8,128)(2,1)S(1)}, bf16[16,128,512]{2,1,0:T(8,128)(2,1)}, u32[]{:S(2)}) copy-start(bf16[16,128,512]{2,1,0:T(8,128)(2,1)} %param.13) | copy-start | bytes 6291460
  6.5 64.2 %all-gather.2.cloned.1.call-start = ((), (), s32[]{:S(2)}) async-start(), calls=%async_computation.1 | async-start | bytes 10616832 | tf_op jit(solution)/shard_map/all_gather | solution.py:80
  7.3 175.1 %reduce-scatter.2.cloned.1.call-start = ((), (), s32[]{:S(2)}) async-start(), calls=%async_computation.2 | async-start | bytes 1146880 | tf_op jit(solution)/shard_map/reduce_scatter | solution.py:100
  12.3 60.0 %copy-start.4 = (bf16[1024,576]{1,0:T(8,128)(2,1)S(1)}, bf16[1024,576]{1,0:T(8,128)(2,1)}, u32[]{:S(2)}) copy-start(bf16[1024,576]{1,0:T(8,128)(2,1)} %pad_maximum_fusion) | copy-start | bytes 3538948
  75.9 1.6 copy-start.1
  80.5 1.3 copy-start.2
  85.4 1.6 copy-start.1
  90.0 1.3 copy-start.2
  95.0 1.6 copy-start.1
  99.6 1.3 copy-start.2
  104.5 1.6 copy-start.1
  109.1 1.3 copy-start.2
  114.0 1.6 copy-start.1
  118.6 1.3 copy-start.2
  123.6 1.6 copy-start.1
  128.2 1.3 copy-start.2
  129.5 2.2 %copy-start.3 = (bf16[16,512,128]{2,1,0:T(8,128)(2,1)S(1)}, bf16[16,512,128]{2,1,0:T(8,128)(2,1)}, u32[]{:S(2)}) copy-start(bf16[16,512,128]{2,1,0:T(8,128)(2,1)} %param.14) | copy-start | bytes 6291460
Sparse Core Ops, SparseCore 0:
  9.2 61.4 all-gather.1
  147.6 34.7 reduce-scatter.1
where the time goes:
time: 190 us; the launch traced here: 189 us
  waiting for transfers between devices  94 us (49%)
  matrix products  55.8 us (29%)
  between operations  14.1 us (7%)
  other arithmetic  12.5 us (7%)
  local copies, waits for them, and re-layouts  12.4 us (7%)
    all_gather x1, waiting for transfers between devices, on_device(): cache_piece = lax.all_gather(latent_cache, 'ctx', axis=1, tiled=True)  58.4 us
    reduce_scatter x1, waiting for transfers between devices, on_device(): lax.psum_scatter(lax.dot_general(w_o, head_out, (((0,), (1,)), ((), ())),...  34.9 us
    dot_general x6, matrix products, block_scores_of(): jnp.dot(query_rows, key_block, preferred_element_type=jnp.float32)  20.6 us
    dot_general x6, matrix products, latent_product(): lax.dot_general(weights.astype(jnp.bfloat16), key_block[:LATENT], (((1,),...  18.1 us
    dot_general x1, matrix products, on_device(): lax.dot_general(w_o, head_out, (((0,), (1,)), ((), ())), preferred_elemen...  13.1 us
    reduce_sum x6, other arithmetic, online_update(): denominator = denominator * decay_factor + jnp.sum(weights, axis=1)  9.27 us
    cond x30, local copies, waits for them, and re-layouts  7.95 us
  transfers between devices with their start and end apart: 2, of which 2 were waited for; matrix products, arithmetic and copies ran while one was open for 2% of the time, Pallas kernels for 0%

commit v1 on v0

--- a/solution.py
+++ b/solution.py
@@ -77,7 +77,12 @@
         jnp.zeros((row_total,), jnp.float32),
         jnp.zeros((row_total, LATENT), jnp.float32),
     )
-    cache_piece = lax.all_gather(latent_cache, "ctx", axis=1, tiled=True)
+    ring = [latent_cache]
+    for hop in range(7):
+        ring.append(lax.ppermute(ring[-1], "ctx", [(dev, (dev + 1) % 8) for dev in range(8)]))
+    cache_piece = jnp.roll(
+        jnp.concatenate(ring[::-1], axis=1), (lax.axis_index("ctx") + 1) * ring[0].shape[1], axis=1
+    )
     span_keys = cache_piece.shape[1]
     step_keys = math.gcd(span_keys, 1024)
 

time: 190 us -> 269 us (1.42)
  waiting for transfers between devices: 94 us -> 143 us
  local copies, waits for them, and re-layouts: 12.4 us -> 39.8 us
    ppermute x0 -> x7, waiting for transfers between devices: none -> 110 us  [on_device(): lax.ppermute(ring[-1], 'ctx', [(dev, (dev + 1) % 8) for dev in range(8)])]
    all_gather x1 -> x0, waiting for transfers between devices: 58.4 us -> none  [on_device(): cache_piece = lax.all_gather(latent_cache, 'ctx', axis=1, tiled=True)]
    unnamed x6 -> x47, local copies, waits for them, and re-layouts: 0.27 us -> 27.2 us
    dynamic_slice x0 -> x1, local copies, waits for them, and re-layouts: none -> 8.62 us  [on_device(): jnp.roll(jnp.concatenate(ring[::-1], axis=1), (lax.axis_index('ctx') + 1)...]
    cond x30 -> x6, local copies, waits for them, and re-layouts: 7.95 us -> 0.02 us
  transfers between devices with their start and end apart: 2 -> 8, of which waited for: 2 -> 8; matrix products, arithmetic and copies ran while one was open for 2% -> 2% of each run, Pallas kernels for 0% -> 0%
where the time goes in v1:
time: 269 us; the launch traced here: 268 us
  waiting for transfers between devices  143 us (53%)
  matrix products  56.1 us (21%)
  local copies, waits for them, and re-layouts  39.8 us (15%)
  between operations  14.2 us (5%)
  other arithmetic  13.8 us (5%)
    ppermute x7, waiting for transfers between devices, on_device(): lax.ppermute(ring[-1], 'ctx', [(dev, (dev + 1) % 8) for dev in range(8)])  110 us
    reduce_scatter x1, waiting for transfers between devices, on_device(): lax.psum_scatter(lax.dot_general(w_o, head_out, (((0,), (1,)), ((), ())),...  32.5 us
    unnamed x47, local copies, waits for them, and re-layouts  27.2 us
    dot_general x6, matrix products, block_scores_of(): jnp.dot(query_rows, key_block, preferred_element_type=jnp.float32)  20.5 us
    dot_general x6, matrix products, latent_product(): lax.dot_general(weights.astype(jnp.bfloat16), key_block[:LATENT], (((1,),...  18.1 us
    dot_general x1, matrix products, on_device(): lax.dot_general(w_o, head_out, (((0,), (1,)), ((), ())), preferred_elemen...  13.2 us
    reduce_sum x6, other arithmetic, online_update(): denominator = denominator * decay_factor + jnp.sum(weights, axis=1)  9.26 us
    dynamic_slice x1, local copies, waits for them, and re-layouts, on_device(): jnp.roll(jnp.concatenate(ring[::-1], axis=1), (lax.axis_index('ctx') + 1)...  8.62 us
  transfers between devices with their start and end apart: 8, of which 8 were waited for; matrix products, arithmetic and copies ran while one was open for 2% of the time, Pallas kernels for 0%

profile of v1, /device:TPU:0, one launch (start us, length us, event | category | flops | bytes accessed | tf_op | source)
XLA Modules:
  0.0 267.9 jit_solution(10075522630338084650)
XLA Ops:
  6.5 0.5 collective-permute-start
  7.0 17.0 %collective-permute-done = bf16[576,1024]{1,0:T(8,128)(2,1)S(1)} collective-permute-done((bf16[576,1024]{1,0:T(8,128)(2,1)}, bf16[576,1024]{1,0:T(8,128)(2,1)S(1)}, u32[]{:S(2)}, u32[]{:S(2)}) %collective-permute-start) | collective-permute-done | bytes 1179680 | tf_op jit(solution)/shard_map/ppermute | solution.py:82
  24.0 16.5 %collective-permute-done.1 = bf16[576,1024]{1,0:T(8,128)(2,1)S(1)} collective-permute-done((bf16[576,1024]{1,0:T(8,128)(2,1)S(1)}, bf16[576,1024]{1,0:T(8,128)(2,1)S(1)}, u32[]{:S(2)}, u32[]{:S(2)}) %collective-permute-start.1) | collective-permute-done | bytes 1179680 | tf_op jit(solution)/shard_map/ppermute | solution.py:82
  40.5 1.0 copy-done.5
  41.6 16.5 %collective-permute-done.2 = bf16[576,1024]{1,0:T(8,128)(2,1)S(1)} collective-permute-done((bf16[576,1024]{1,0:T(8,128)(2,1)S(1)}, bf16[576,1024]{1,0:T(8,128)(2,1)S(1)}, u32[]{:S(2)}, u32[]{:S(2)}) %collective-permute-start.2) | collective-permute-done | bytes 1179680 | tf_op jit(solution)/shard_map/ppermute | solution.py:82
  58.1 1.0 copy-done.7
  59.1 16.5 %collective-permute-done.3 = bf16[576,1024]{1,0:T(8,128)(2,1)S(1)} collective-permute-done((bf16[576,1024]{1,0:T(8,128)(2,1)S(1)}, bf16[576,1024]{1,0:T(8,128)(2,1)S(1)}, u32[]{:S(2)}, u32[]{:S(2)}) %collective-permute-start.3) | collective-permute-done | bytes 1179680 | tf_op jit(solution)/shard_map/ppermute | solution.py:82
  75.7 1.1 copy-done.9
  76.8 16.5 %collective-permute-done.4 = bf16[576,1024]{1,0:T(8,128)(2,1)S(1)} collective-permute-done((bf16[576,1024]{1,0:T(8,128)(2,1)S(1)}, bf16[576,1024]{1,0:T(8,128)(2,1)S(1)}, u32[]{:S(2)}, u32[]{:S(2)}) %collective-permute-start.4) | collective-permute-done | bytes 1179680 | tf_op jit(solution)/shard_map/ppermute | solution.py:82
  93.3 1.0 copy-done.11
  94.3 16.6 %collective-permute-done.5 = bf16[576,1024]{1,0:T(8,128)(2,1)} collective-permute-done((bf16[576,1024]{1,0:T(8,128)(2,1)S(1)}, bf16[576,1024]{1,0:T(8,128)(2,1)}, u32[]{:S(2)}, u32[]{:S(2)}) %collective-permute-start.5) | collective-permute-done | bytes 1179680 | tf_op jit(solution)/shard_map/ppermute | solution.py:82
  111.6 1.4 fusion.20
  113.0 1.5 copy.12
  114.8 2.6 pad_maximum_fusion
  117.3 10.5 %collective-permute-done.6 = bf16[576,1024]{1,0:T(8,128)(2,1)} collective-permute-done((bf16[576,1024]{1,0:T(8,128)(2,1)}, bf16[576,1024]{1,0:T(8,128)(2,1)}, u32[]{:S(2)}, u32[]{:S(2)}) %collective-permute-start.6) | collective-permute-done | bytes 1179680 | tf_op jit(solution)/shard_map/ppermute | solution.py:82
  127.8 2.4 constant_dynamic-update-slice_fusion.15
  130.2 2.4 constant_dynamic-update-slice_fusion.14
  132.6 1.1 constant_dynamic-update-slice_fusion.13
  133.7 1.1 constant_dynamic-update-slice_fusion.12
  134.8 1.1 constant_dynamic-update-slice_fusion.11
  135.9 1.1 constant_dynamic-update-slice_fusion.10
  137.0 1.1 constant_dynamic-update-slice_fusion.9
  138.1 1.1 constant_dynamic-update-slice_fusion.8
  139.2 2.4 constant_dynamic-update-slice_fusion.7
  141.6 2.4 constant_dynamic-update-slice_fusion.6
  144.0 1.1 constant_dynamic-update-slice_fusion.5
  145.1 1.1 constant_dynamic-update-slice_fusion.4
  146.2 1.1 constant_dynamic-update-slice_fusion.3
  147.3 1.1 constant_dynamic-update-slice_fusion.2
  148.4 1.1 constant_dynamic-update-slice_fusion.1
  149.5 1.1 constant_dynamic-update-slice_fusion
  150.6 8.6 %constant_dynamic-slice_fusion = bf16[576,8192]{1,0:T(8,128)(2,1)} fusion(bf16[576,16384]{1,0:T(8,128)(2,1)} %constant_dynamic-update-slice_fusion, s32[]{:T(128)S(6)} %select_n.35), kind=kLoop, calls=%fused_computation.53 | loop fusion | bytes 18874372 | tf_op jit(solution)/shard_map/jit(_roll_dynamic)/dynamic_slice | solution.py:83
  159.2 0.2 broadcast_in_dim.29
  159.5 49.7 %while.18 = (s32[]{:T(128)}, f32[1024]{0:T(1024)S(1)}, f32[1024]{0:T(1024)S(1)}, f32[1024,512]{1,0:T(8,128)S(1)}, s32[]{:T(128)}, /*index=5*/bf16[576,8192]{1,0:...) while((s32[]{:T(128)}, f32[1024]{0:T(1024)S(1)}, ...), condition=%wide.region_5.6_spmd.clone, body=%wide.region_0.5_spmd.clone.sunk | while | flops 2299530240 | bytes 20292124 | solution.py:101
  159.7 8.2 %conditional.3 = ((f32[1024]{0:T(1024)S(1)}, f32[1024]{0:T(1024)S(1)}, f32[1024,512]{1,0:T(8,128)S(1)})) conditional(s32[]{:T(128)} %convert_element_type.82, (f32[1024]{0:T(1024)S(1)}, f32[1024]{0:T(1024)S(1)}, f32[1024,512]{1,0:T(8,128)S(1)}) %tuple.50, (s32[]{:T(128)}, s32[64]{0:T(128)S(1)}, bf16[576,8192]{1,0:T(8,128)(2,1)}, ...), branch_computations={%region_1.1_spmd, %region_2.4_spmd} | conditional | flops 2299530240 | bytes 20291918 | solution.py:92
  159.9 3.4 %fusion.2 = (f32[1024]{0:T(1024)S(1)}, f32[1024,1024]{1,0:T(8,128)S(1)}) fusion(s32[1024]{0:T(1024)S(1)} %le.27, s32[1024]{0:T(1024)S(1)} %iota_add_fusion, bf16[1024,576]{1,0:T(8,128)(2,1)S(1)} %get-tuple-element.214, bf16[576,8192]{1,0:T(8,128)(2,1)} %get-tuple-element.213, s32[]{:T(128)S(6)} %select_n.29), kind=kOutput, calls=%fused_computation.3 | convolution fusion | flops 1212152832 | bytes 6565892 | tf_op jit(solution)/shard_map/while/body/eval_jaxpr/cond/branch_1_fun/dot_general | solution.py:30
  163.3 1.5 fusion.4
  164.9 3.0 %multiply_add_fusion = f32[1024,512]{1,0:T(8,128)S(1)} fusion(f32[1024,512]{1,0:T(8,128)S(1)} %get-tuple-element.216, f32[1024,1024]{1,0:T(8,128)S(1)} %get-tuple-element.275, f32[1024]{0:T(1024)S(1)} %max.4, s32[1024]{0:T(1024)S(1)} %le.27, s32[1024]{0:T(1024)S(1)} %iota_add_fusion, bf16[576,8192]{1,0:T(8,128)(2,1)} %get-tuple-element.213, ...), kind=kOutput, calls=%fused_computation.6 | convolution fusion | flops 1081081856 | bytes 9453572 | tf_op jit(solution)/shard_map/while/body/eval_jaxpr/cond/branch_1_fun/dot_general | solution.py:37
  167.9 8.2 %conditional.3 = ((f32[1024]{0:T(1024)S(1)}, f32[1024]{0:T(1024)S(1)}, f32[1024,512]{1,0:T(8,128)S(1)})) conditional(s32[]{:T(128)} %convert_element_type.82, (f32[1024]{0:T(1024)S(1)}, f32[1024]{0:T(1024)S(1)}, f32[1024,512]{1,0:T(8,128)S(1)}) %tuple.50, (s32[]{:T(128)}, s32[64]{0:T(128)S(1)}, bf16[576,8192]{1,0:T(8,128)(2,1)}, ...), branch_computations={%region_1.1_spmd, %region_2.4_spmd} | conditional | flops 2299530240 | bytes 20291918 | solution.py:92
  168.1 3.4 %fusion.2 = (f32[1024]{0:T(1024)S(1)}, f32[1024,1024]{1,0:T(8,128)S(1)}) fusion(s32[1024]{0:T(1024)S(1)} %le.27, s32[1024]{0:T(1024)S(1)} %iota_add_fusion, bf16[1024,576]{1,0:T(8,128)(2,1)S(1)} %get-tuple-element.214, bf16[576,8192]{1,0:T(8,128)(2,1)} %get-tuple-element.213, s32[]{:T(128)S(6)} %select_n.29), kind=kOutput, calls=%fused_computation.3 | convolution fusion | flops 1212152832 | bytes 6565892 | tf_op jit(solution)/shard_map/while/body/eval_jaxpr/cond/branch_1_fun/dot_general | solution.py:30
  171.6 1.5 fusion.4
  173.1 3.0 %multiply_add_fusion = f32[1024,512]{1,0:T(8,128)S(1)} fusion(f32[1024,512]{1,0:T(8,128)S(1)} %get-tuple-element.216, f32[1024,1024]{1,0:T(8,128)S(1)} %get-tuple-element.275, f32[1024]{0:T(1024)S(1)} %max.4, s32[1024]{0:T(1024)S(1)} %le.27, s32[1024]{0:T(1024)S(1)} %iota_add_fusion, bf16[576,8192]{1,0:T(8,128)(2,1)} %get-tuple-element.213, ...), kind=kOutput, calls=%fused_computation.6 | convolution fusion | flops 1081081856 | bytes 9453572 | tf_op jit(solution)/shard_map/while/body/eval_jaxpr/cond/branch_1_fun/dot_general | solution.py:37
  176.2 8.2 %conditional.3 = ((f32[1024]{0:T(1024)S(1)}, f32[1024]{0:T(1024)S(1)}, f32[1024,512]{1,0:T(8,128)S(1)})) conditional(s32[]{:T(128)} %convert_element_type.82, (f32[1024]{0:T(1024)S(1)}, f32[1024]{0:T(1024)S(1)}, f32[1024,512]{1,0:T(8,128)S(1)}) %tuple.50, (s32[]{:T(128)}, s32[64]{0:T(128)S(1)}, bf16[576,8192]{1,0:T(8,128)(2,1)}, ...), branch_computations={%region_1.1_spmd, %region_2.4_spmd} | conditional | flops 2299530240 | bytes 20291918 | solution.py:92
  176.4 3.4 %fusion.2 = (f32[1024]{0:T(1024)S(1)}, f32[1024,1024]{1,0:T(8,128)S(1)}) fusion(s32[1024]{0:T(1024)S(1)} %le.27, s32[1024]{0:T(1024)S(1)} %iota_add_fusion, bf16[1024,576]{1,0:T(8,128)(2,1)S(1)} %get-tuple-element.214, bf16[576,8192]{1,0:T(8,128)(2,1)} %get-tuple-element.213, s32[]{:T(128)S(6)} %select_n.29), kind=kOutput, calls=%fused_computation.3 | convolution fusion | flops 1212152832 | bytes 6565892 | tf_op jit(solution)/shard_map/while/body/eval_jaxpr/cond/branch_1_fun/dot_general | solution.py:30
  179.8 1.5 fusion.4
  181.4 3.0 %multiply_add_fusion = f32[1024,512]{1,0:T(8,128)S(1)} fusion(f32[1024,512]{1,0:T(8,128)S(1)} %get-tuple-element.216, f32[1024,1024]{1,0:T(8,128)S(1)} %get-tuple-element.275, f32[1024]{0:T(1024)S(1)} %max.4, s32[1024]{0:T(1024)S(1)} %le.27, s32[1024]{0:T(1024)S(1)} %iota_add_fusion, bf16[576,8192]{1,0:T(8,128)(2,1)} %get-tuple-element.213, ...), kind=kOutput, calls=%fused_computation.6 | convolution fusion | flops 1081081856 | bytes 9453572 | tf_op jit(solution)/shard_map/while/body/eval_jaxpr/cond/branch_1_fun/dot_general | solution.py:37
  184.4 8.2 %conditional.3 = ((f32[1024]{0:T(1024)S(1)}, f32[1024]{0:T(1024)S(1)}, f32[1024,512]{1,0:T(8,128)S(1)})) conditional(s32[]{:T(128)} %convert_element_type.82, (f32[1024]{0:T(1024)S(1)}, f32[1024]{0:T(1024)S(1)}, f32[1024,512]{1,0:T(8,128)S(1)}) %tuple.50, (s32[]{:T(128)}, s32[64]{0:T(128)S(1)}, bf16[576,8192]{1,0:T(8,128)(2,1)}, ...), branch_computations={%region_1.1_spmd, %region_2.4_spmd} | conditional | flops 2299530240 | bytes 20291918 | solution.py:92
  184.6 3.4 %fusion.2 = (f32[1024]{0:T(1024)S(1)}, f32[1024,1024]{1,0:T(8,128)S(1)}) fusion(s32[1024]{0:T(1024)S(1)} %le.27, s32[1024]{0:T(1024)S(1)} %iota_add_fusion, bf16[1024,576]{1,0:T(8,128)(2,1)S(1)} %get-tuple-element.214, bf16[576,8192]{1,0:T(8,128)(2,1)} %get-tuple-element.213, s32[]{:T(128)S(6)} %select_n.29), kind=kOutput, calls=%fused_computation.3 | convolution fusion | flops 1212152832 | bytes 6565892 | tf_op jit(solution)/shard_map/while/body/eval_jaxpr/cond/branch_1_fun/dot_general | solution.py:30
  188.0 1.5 fusion.4
  189.6 3.0 %multiply_add_fusion = f32[1024,512]{1,0:T(8,128)S(1)} fusion(f32[1024,512]{1,0:T(8,128)S(1)} %get-tuple-element.216, f32[1024,1024]{1,0:T(8,128)S(1)} %get-tuple-element.275, f32[1024]{0:T(1024)S(1)} %max.4, s32[1024]{0:T(1024)S(1)} %le.27, s32[1024]{0:T(1024)S(1)} %iota_add_fusion, bf16[576,8192]{1,0:T(8,128)(2,1)} %get-tuple-element.213, ...), kind=kOutput, calls=%fused_computation.6 | convolution fusion | flops 1081081856 | bytes 9453572 | tf_op jit(solution)/shard_map/while/body/eval_jaxpr/cond/branch_1_fun/dot_general | solution.py:37
  192.7 8.2 %conditional.3 = ((f32[1024]{0:T(1024)S(1)}, f32[1024]{0:T(1024)S(1)}, f32[1024,512]{1,0:T(8,128)S(1)})) conditional(s32[]{:T(128)} %convert_element_type.82, (f32[1024]{0:T(1024)S(1)}, f32[1024]{0:T(1024)S(1)}, f32[1024,512]{1,0:T(8,128)S(1)}) %tuple.50, (s32[]{:T(128)}, s32[64]{0:T(128)S(1)}, bf16[576,8192]{1,0:T(8,128)(2,1)}, ...), branch_computations={%region_1.1_spmd, %region_2.4_spmd} | conditional | flops 2299530240 | bytes 20291918 | solution.py:92
  192.8 3.4 %fusion.2 = (f32[1024]{0:T(1024)S(1)}, f32[1024,1024]{1,0:T(8,128)S(1)}) fusion(s32[1024]{0:T(1024)S(1)} %le.27, s32[1024]{0:T(1024)S(1)} %iota_add_fusion, bf16[1024,576]{1,0:T(8,128)(2,1)S(1)} %get-tuple-element.214, bf16[576,8192]{1,0:T(8,128)(2,1)} %get-tuple-element.213, s32[]{:T(128)S(6)} %select_n.29), kind=kOutput, calls=%fused_computation.3 | convolution fusion | flops 1212152832 | bytes 6565892 | tf_op jit(solution)/shard_map/while/body/eval_jaxpr/cond/branch_1_fun/dot_general | solution.py:30
  196.3 1.5 fusion.4
  197.9 3.0 %multiply_add_fusion = f32[1024,512]{1,0:T(8,128)S(1)} fusion(f32[1024,512]{1,0:T(8,128)S(1)} %get-tuple-element.216, f32[1024,1024]{1,0:T(8,128)S(1)} %get-tuple-element.275, f32[1024]{0:T(1024)S(1)} %max.4, s32[1024]{0:T(1024)S(1)} %le.27, s32[1024]{0:T(1024)S(1)} %iota_add_fusion, bf16[576,8192]{1,0:T(8,128)(2,1)} %get-tuple-element.213, ...), kind=kOutput, calls=%fused_computation.6 | convolution fusion | flops 1081081856 | bytes 9453572 | tf_op jit(solution)/shard_map/while/body/eval_jaxpr/cond/branch_1_fun/dot_general | solution.py:37
  200.9 8.2 %conditional.3 = ((f32[1024]{0:T(1024)S(1)}, f32[1024]{0:T(1024)S(1)}, f32[1024,512]{1,0:T(8,128)S(1)})) conditional(s32[]{:T(128)} %convert_element_type.82, (f32[1024]{0:T(1024)S(1)}, f32[1024]{0:T(1024)S(1)}, f32[1024,512]{1,0:T(8,128)S(1)}) %tuple.50, (s32[]{:T(128)}, s32[64]{0:T(128)S(1)}, bf16[576,8192]{1,0:T(8,128)(2,1)}, ...), branch_computations={%region_1.1_spmd, %region_2.4_spmd} | conditional | flops 2299530240 | bytes 20291918 | solution.py:92
  201.1 3.4 %fusion.2 = (f32[1024]{0:T(1024)S(1)}, f32[1024,1024]{1,0:T(8,128)S(1)}) fusion(s32[1024]{0:T(1024)S(1)} %le.27, s32[1024]{0:T(1024)S(1)} %iota_add_fusion, bf16[1024,576]{1,0:T(8,128)(2,1)S(1)} %get-tuple-element.214, bf16[576,8192]{1,0:T(8,128)(2,1)} %get-tuple-element.213, s32[]{:T(128)S(6)} %select_n.29), kind=kOutput, calls=%fused_computation.3 | convolution fusion | flops 1212152832 | bytes 6565892 | tf_op jit(solution)/shard_map/while/body/eval_jaxpr/cond/branch_1_fun/dot_general | solution.py:30
  204.5 1.5 fusion.4
  206.1 3.0 %multiply_add_fusion = f32[1024,512]{1,0:T(8,128)S(1)} fusion(f32[1024,512]{1,0:T(8,128)S(1)} %get-tuple-element.216, f32[1024,1024]{1,0:T(8,128)S(1)} %get-tuple-element.275, f32[1024]{0:T(1024)S(1)} %max.4, s32[1024]{0:T(1024)S(1)} %le.27, s32[1024]{0:T(1024)S(1)} %iota_add_fusion, bf16[576,8192]{1,0:T(8,128)(2,1)} %get-tuple-element.213, ...), kind=kOutput, calls=%fused_computation.6 | convolution fusion | flops 1081081856 | bytes 9453572 | tf_op jit(solution)/shard_map/while/body/eval_jaxpr/cond/branch_1_fun/dot_general | solution.py:37
  209.2 1.3 copy-done.2
  210.6 1.9 broadcast_divide_fusion
  212.4 1.4 fusion.19
  213.9 1.5 fusion.22
  215.3 13.2 %fusion.18 = bf16[7168,64]{0,1:T(8,128)(2,1)} fusion(bf16[2048,7168]{1,0:T(8,128)(2,1)} %param.15, bf16[16,8,8,128]{3,2,1,0:T(8,128)(2,1)S(1)} %fusion.22), kind=kOutput, calls=%fused_computation.21 | convolution fusion | flops 1879506944 | bytes 30539776 | tf_op jit(solution)/shard_map/dot_general | solution.py:106
  228.6 32.5 %reduce-scatter.2.cloned.1.call-done = bf16[1792,64]{0,1:T(8,128)(2,1)} async-done(((bf16[7168,64]{0,1:T(8,128)(2,1)}), bf16[1792,64]{0,1:T(8,128)(2,1)}) %reduce-scatter.2.cloned.1.call-update) | async-done | bytes 229392 | tf_op jit(solution)/shard_map/reduce_scatter | solution.py:105
  (77 shorter events, 1.3 us)
Async XLA Ops:
  6.5 105.1 %copy-start = (bf16[16,128,512]{2,1,0:T(8,128)(2,1)S(1)}, bf16[16,128,512]{2,1,0:T(8,128)(2,1)}, u32[]{:S(2)}) copy-start(bf16[16,128,512]{2,1,0:T(8,128)(2,1)} %param.13) | copy-start | bytes 6291460
  6.5 108.0 %copy-start.15 = (bf16[64,1024]{1,0:T(8,128)(2,1)S(1)}, bf16[64,1024]{1,0:T(8,128)(2,1)}, u32[]{:S(2)}) copy-start(bf16[64,1024]{1,0:T(8,128)(2,1)} %param.12) | copy-start | bytes 393220
  6.5 254.5 %reduce-scatter.2.cloned.1.call-start = ((), (), s32[]{:S(2)}) async-start(), calls=%async_computation.1 | async-start | bytes 1146880 | tf_op jit(solution)/shard_map/reduce_scatter | solution.py:105
  6.5 17.5 %collective-permute-start = (bf16[576,1024]{1,0:T(8,128)(2,1)}, bf16[576,1024]{1,0:T(8,128)(2,1)S(1)}, u32[]{:S(2)}, u32[]{:S(2)}) collective-permute-start(bf16[576,1024]{1,0:T(8,128)(2,1)} %param.16), channel_id=1, source_target_pairs={{0,4},{4,8},{8,12},{12,16},{16,20},{20,24},{24,28},{28,0},{1,5},{5... | collective-permute-start | bytes 3538952 | tf_op jit(solution)/shard_map/ppermute | solution.py:82
  24.0 16.5 %collective-permute-start.1 = (bf16[576,1024]{1,0:T(8,128)(2,1)S(1)}, bf16[576,1024]{1,0:T(8,128)(2,1)S(1)}, u32[]{:S(2)}, u32[]{:S(2)}) collective-permute-start(bf16[576,1024]{1,0:T(8,128)(2,1)S(1)} %collective-permute-done), channel_id=1, source_target_pairs={{0,4},{4,8},{8,12},{12,16},{16,20},{20,24},{24,28},{28,0},{1,5},{5... | collective-permute-start | bytes 3538952 | tf_op jit(solution)/shard_map/ppermute | solution.py:82
  40.5 1.0 copy-start.5
  41.6 16.5 %collective-permute-start.2 = (bf16[576,1024]{1,0:T(8,128)(2,1)S(1)}, bf16[576,1024]{1,0:T(8,128)(2,1)S(1)}, u32[]{:S(2)}, u32[]{:S(2)}) collective-permute-start(bf16[576,1024]{1,0:T(8,128)(2,1)S(1)} %collective-permute-done.1), channel_id=1, source_target_pairs={{0,4},{4,8},{8,12},{12,16},{16,20},{20,24},{24,28},{28,0},{1,5},{5... | collective-permute-start | bytes 3538952 | tf_op jit(solution)/shard_map/ppermute | solution.py:82
  58.1 1.0 copy-start.7
  59.1 16.5 %collective-permute-start.3 = (bf16[576,1024]{1,0:T(8,128)(2,1)S(1)}, bf16[576,1024]{1,0:T(8,128)(2,1)S(1)}, u32[]{:S(2)}, u32[]{:S(2)}) collective-permute-start(bf16[576,1024]{1,0:T(8,128)(2,1)S(1)} %collective-permute-done.2), channel_id=1, source_target_pairs={{0,4},{4,8},{8,12},{12,16},{16,20},{20,24},{24,28},{28,0},{1,5},{5... | collective-permute-start | bytes 3538952 | tf_op jit(solution)/shard_map/ppermute | solution.py:82
  75.7 1.1 copy-start.9
  76.8 16.5 %collective-permute-start.4 = (bf16[576,1024]{1,0:T(8,128)(2,1)S(1)}, bf16[576,1024]{1,0:T(8,128)(2,1)S(1)}, u32[]{:S(2)}, u32[]{:S(2)}) collective-permute-start(bf16[576,1024]{1,0:T(8,128)(2,1)S(1)} %collective-permute-done.3), channel_id=1, source_target_pairs={{0,4},{4,8},{8,12},{12,16},{16,20},{20,24},{24,28},{28,0},{1,5},{5... | collective-permute-start | bytes 3538952 | tf_op jit(solution)/shard_map/ppermute | solution.py:82
  93.3 1.0 copy-start.11
  94.3 16.6 %collective-permute-start.5 = (bf16[576,1024]{1,0:T(8,128)(2,1)S(1)}, bf16[576,1024]{1,0:T(8,128)(2,1)}, u32[]{:S(2)}, u32[]{:S(2)}) collective-permute-start(bf16[576,1024]{1,0:T(8,128)(2,1)S(1)} %collective-permute-done.4), channel_id=1, source_target_pairs={{0,4},{4,8},{8,12},{12,16},{16,20},{20,24},{24,28},{28,0},{1,5},{5... | collective-permute-start | bytes 3538952 | tf_op jit(solution)/shard_map/ppermute | solution.py:82
  111.0 16.8 %collective-permute-start.6 = (bf16[576,1024]{1,0:T(8,128)(2,1)}, bf16[576,1024]{1,0:T(8,128)(2,1)}, u32[]{:S(2)}, u32[]{:S(2)}) collective-permute-start(bf16[576,1024]{1,0:T(8,128)(2,1)} %collective-permute-done.5), channel_id=1, source_target_pairs={{0,4},{4,8},{8,12},{12,16},{16,20},{20,24},{24,28},{28,0},{1,5},{5... | collective-permute-start | bytes 3538952 | tf_op jit(solution)/shard_map/ppermute | solution.py:82
  114.6 18.1 %copy-start.12 = (bf16[576,1024]{1,0:T(8,128)(2,1)S(1)}, bf16[576,1024]{1,0:T(8,128)(2,1)}, u32[]{:S(2)}) copy-start(bf16[576,1024]{1,0:T(8,128)(2,1)} %copy-done.11) | copy-start | bytes 3538948
  114.8 18.9 %copy-start.10 = (bf16[576,1024]{1,0:T(8,128)(2,1)S(1)}, bf16[576,1024]{1,0:T(8,128)(2,1)}, u32[]{:S(2)}) copy-start(bf16[576,1024]{1,0:T(8,128)(2,1)} %copy-done.9) | copy-start | bytes 3538948
  117.3 17.5 %copy-start.8 = (bf16[576,1024]{1,0:T(8,128)(2,1)S(1)}, bf16[576,1024]{1,0:T(8,128)(2,1)}, u32[]{:S(2)}) copy-start(bf16[576,1024]{1,0:T(8,128)(2,1)} %copy-done.7) | copy-start | bytes 3538948
  130.2 5.7 %copy-start.6 = (bf16[576,1024]{1,0:T(8,128)(2,1)S(1)}, bf16[576,1024]{1,0:T(8,128)(2,1)}, u32[]{:S(2)}) copy-start(bf16[576,1024]{1,0:T(8,128)(2,1)} %copy-done.5) | copy-start | bytes 3538948
  133.7 4.4 %copy-start.4 = (bf16[576,1024]{1,0:T(8,128)(2,1)S(1)}, bf16[576,1024]{1,0:T(8,128)(2,1)}, u32[]{:S(2)}) copy-start(bf16[576,1024]{1,0:T(8,128)(2,1)} %param.16) | copy-start | bytes 3538948
  137.0 7.0 %copy-start.13 = (bf16[576,1024]{1,0:T(8,128)(2,1)S(1)}, bf16[576,1024]{1,0:T(8,128)(2,1)}, u32[]{:S(2)}) copy-start(bf16[576,1024]{1,0:T(8,128)(2,1)} %copy-done.11) | copy-start | bytes 3538948
  150.6 8.9 %copy-start.14 = (bf16[1024,576]{1,0:T(8,128)(2,1)S(1)}, bf16[1024,576]{1,0:T(8,128)(2,1)}, u32[]{:S(2)}) copy-start(bf16[1024,576]{1,0:T(8,128)(2,1)} %pad_maximum_fusion) | copy-start | bytes 3538948
  209.2 1.3 copy-start.2
  209.2 3.2 %copy-start.3 = (bf16[16,512,128]{2,1,0:T(8,128)(2,1)S(1)}, bf16[16,512,128]{2,1,0:T(8,128)(2,1)}, u32[]{:S(2)}) copy-start(bf16[16,512,128]{2,1,0:T(8,128)(2,1)} %param.14) | copy-start | bytes 6291460
  215.3 45.7 %copy-start.1 = (bf16[16,128,512]{2,1,0:T(8,128)(2,1)S(1)}, bf16[16,128,512]{2,1,0:T(8,128)(2,1)}, u32[]{:S(2)}) copy-start(bf16[16,128,512]{2,1,0:T(8,128)(2,1)} %param.13) | copy-start | bytes 6291460
Sparse Core Ops, SparseCore 0:
  228.7 32.2 reduce-scatter.1
